TPU v7x, 32 devices: a whole 2x2x4 slice. The times are simulated.
32 devices in a mesh: dp: 4 (over y, x), expert: 8 (over z, core).
Axes of the slice: x: 2, y: 2, z: 4, core: 2. Of those that a mesh axis runs over, the one named last changes fastest.
Arguments:
- tokens: bfloat16 [256, 4096], P(('dp', 'expert')), may hold values from -6 to 6
- route_weight: float32 [256, 8], P(('dp', 'expert')), may hold values from 0.1 to 1
- expert_ids: int32 [256, 8], P(('dp', 'expert')), may hold values from 0 to 15, all different within a row; in each aligned block of 8 rows (0 to 7, 8 to 15, ...) at most 8 rows name the same one
- placement: int32 [16], replicated, may hold values from 0 to 15, each once
- pair_step: int32 [8], replicated, may hold values from 0 to 1
- move_slot: int32 [8], replicated, may hold values from 0 to 1
- expert_weights: bfloat16 [16, 3, 4096, 1024], P('expert', None, None, 'dp'), may hold values from -0.375 to 0.375
Outputs:
- mixed: bfloat16 [256, 4096], P(('dp', 'expert'))
- moved_weights: bfloat16 [8, 3, 4096, 1024], P('expert', None, None, 'dp')
Inputs may be any that keep to these rules, and one draw needn't show every extreme that they name: `expert_ids`: each row names 8 different experts. Among the rows of one device (aligned blocks of 8 rows, in the order of the tokens) no expert is named more than 8 times, a bound that some block reaches. A permutation of the slots: expert x is held in slot placement[x], which belongs to index placement[x] // 2 of expert.
All inputs are finite; a program needn't handle non-finite values.
Results may differ from a plain program's by a relative error of at most 0.012.
Values may be sent and summed in bfloat16 or wider, within the bound.
A program may use at most 128 MiB of HBM per device.

v0:
```python
import jax
import jax.numpy as jnp
from jax import lax
from jax.sharding import PartitionSpec as P


def swapped(value, axis, bit):
    mask = 2**bit
    pairs = [(source, source ^ mask) for source in range(lax.axis_size(axis))]
    return lax.ppermute(value, axis, pairs)


def pair_offsets(flags):
    count = flags.shape[0]
    columns = jnp.arange(count, dtype=jnp.int32)
    joined = jnp.repeat(jnp.sum(flags.reshape(-1, 2), axis=1) > 0, 2)
    return jnp.where(joined, 1 - 2 * (columns % 2), 0)


def route_slots(chosen, slot_table, capacity, experts):
    flat_ids = chosen.reshape(-1)
    matches = (flat_ids[:, None] == jnp.arange(experts, dtype=jnp.int32)[None, :]).astype(jnp.int32)
    position = jnp.sum(matches * (jnp.cumsum(matches, axis=0) - 1), axis=1)
    slot_ids = jnp.sum(matches * slot_table[None, :], axis=1)
    return slot_ids * capacity + position


def dispatch_rows(flat_slots, token_rows, count, per_token):
    matches = (jnp.arange(count, dtype=jnp.int32)[:, None] == flat_slots[None, :]).astype(jnp.int32)
    select = jnp.sum(matches.reshape(count, token_rows.shape[0], per_token), axis=2).astype(
        jnp.bfloat16
    )
    return jnp.dot(select, token_rows, preferred_element_type=jnp.float32).astype(jnp.bfloat16)


def placement_after(placement, pair_offset, move_slot, exp_col):
    n_col = pair_offset.shape[0]
    columns = jnp.arange(n_col, dtype=jnp.int32)
    home_col = placement // exp_col
    home_pos = placement % exp_col
    at_home = (home_col[:, None] == columns[None, :]).astype(jnp.int32)
    shift_by = jnp.sum(at_home * pair_offset[None, :], axis=1)
    home_moving = jnp.sum(at_home * move_slot[None, :], axis=1)
    target_col = home_col + shift_by
    at_target = (target_col[:, None] == columns[None, :]).astype(jnp.int32)
    target_pos = jnp.sum(at_target * move_slot[None, :], axis=1)
    leaves = (shift_by != 0) & (home_pos == home_moving)
    return jnp.where(leaves, target_col * exp_col + target_pos, placement)


def expert_partial(row_data, weights):
    pair_act = jnp.einsum(
        "ajcd,jkdh->ajckh", row_data, weights[:, :2], preferred_element_type=jnp.float32
    )
    hidden = (jax.nn.silu(pair_act[:, :, :, 0]) * pair_act[:, :, :, 1]).astype(jnp.bfloat16)
    return jnp.einsum("ajch,jdh->ajcd", hidden, weights[:, 2], preferred_element_type=jnp.float32)


def body(tokens, route_weight, expert_ids, placement, pair_step, move_slot, expert_weights):
    exp_col = expert_weights.shape[0]
    n_col = lax.axis_size("expert")
    experts = exp_col * n_col
    tok_dev, top_k = expert_ids.shape
    model_width = tokens.shape[1]
    capacity = 2 * ((tok_dev * top_k + experts - 1) // experts)
    column = lax.axis_index("expert")
    pair_offset = pair_offsets(pair_step)
    step_here = lax.dynamic_index_in_dim(pair_offset, column, 0, keepdims=False)
    moving = lax.dynamic_index_in_dim(move_slot, column, 0, keepdims=False)
    moving_block = lax.dynamic_slice_in_dim(expert_weights, moving, 1, 0)
    partner_block = swapped(moving_block, "expert", 0)
    received = jnp.where(step_here != 0, partner_block, moving_block)
    slot_table = placement_after(placement, pair_offset, move_slot, exp_col)
    weights = lax.dynamic_update_slice_in_dim(expert_weights, received, moving, 0)
    destination = route_slots(expert_ids, slot_table, capacity, experts)
    outgoing = dispatch_rows(destination, tokens, experts * capacity, top_k)
    outgoing = outgoing.reshape(n_col, exp_col, capacity, model_width)
    arrived = lax.all_to_all(outgoing, "expert", split_axis=0, concat_axis=0, tiled=True)
    term_rows = expert_partial(lax.all_gather(arrived, "dp", axis=0, tiled=True), weights)
    summed = lax.psum_scatter(term_rows.astype(jnp.bfloat16), "dp", scatter_dimension=0, tiled=True)
    returned = lax.all_to_all(summed, "expert", split_axis=0, concat_axis=0, tiled=True)
    row_data = returned.reshape(experts * capacity, model_width)
    picked = jnp.take(row_data, destination, axis=0).reshape(tok_dev, top_k, model_width)
    mixed = jnp.sum(route_weight[:, :, None] * picked.astype(jnp.float32), axis=1)
    return (mixed.astype(jnp.bfloat16), received)


def solution(mesh):
    in_specs = (
        P(("dp", "expert"), None),
        P(("dp", "expert"), None),
        P(("dp", "expert"), None),
        P(),
        P(),
        P(),
        P("expert", None, None, "dp"),
    )
    out_specs = (P(("dp", "expert"), None), P("expert", None, None, "dp"))
    return jax.shard_map(body, mesh=mesh, in_specs=in_specs, out_specs=out_specs, check_vma=False)
```

profile of v0, /device:TPU:0, one launch (start us, length us, event | category | flops | bytes accessed | tf_op | source)
XLA Modules:
  0.0 265.9 jit_solution(1814925716669756859)
XLA Ops:
  7.2 0.0 copy-start
  7.2 0.0 copy-start.2
  7.2 0.0 copy-start.5
  7.2 0.0 copy-start.3
  7.2 0.0 copy-start.4
  7.2 10.4 %copy.29 = bf16[2,3,4096,256]{3,2,1,0:T(8,128)(2,1)} copy(bf16[2,3,4096,256]{3,2,1,0:T(8,128)(2,1)} %param.13) | data formatting | bytes 25165824
  17.7 0.0 copy-done.3
  17.7 0.1 reshape.100
  17.8 0.1 reduce_sum.72
  17.9 0.1 broadcast_in_dim.11
  18.0 0.1 reshape.101
  18.1 0.0 copy-done.5
  18.1 0.1 select_reduce_fusion.4
  18.2 0.0 copy-done.2
  18.2 0.1 eq.62
  18.3 0.1 fusion.10
  18.3 0.1 reduce_window_sum.11
  18.4 0.1 select_reduce_fusion.2
  18.5 0.2 select_reduce_fusion.1
  18.7 0.1 add.89
  18.8 0.1 convert_reduce_fusion
  18.9 1.5 convolution_convert_fusion.1
  20.4 6.3 %all-to-all-start = ((bf16[8,2,8,4096]{3,2,1,0:T(8,128)(2,1)}), bf16[8,2,8,4096]{3,2,1,0:T(8,128)(2,1)S(1)}, u32[]{:S(2)}, u32[]{:S(2)}) async-start(bf16[8,2,8,4096]{3,2,1,0:T(8,128)(2,1)} %bitcast.7), calls=%async_computation | async-start | bytes 2097152 | tf_op jit(solution)/shard_map/all_to_all | solution.py:78
  26.7 0.0 all-gather.2.cloned.1.call-start
  26.8 0.6 dynamic_slice.11
  29.3 5.9 %constant_dynamic-slice_fusion.1 = bf16[1,3,4096,256]{3,2,1,0:T(8,128)(2,1)} fusion(bf16[2,3,4096,256]{3,2,1,0:T(8,128)(2,1)} %copy.29, s32[]{:T(128)S(6)} %select_n.80), kind=kLoop, calls=%fused_computation.47 | loop fusion | bytes 12582916 | tf_op jit(solution)/shard_map/dynamic_slice | solution.py:70
  35.2 0.5 collective-permute-start
  35.6 17.7 %all-to-all-done = bf16[8,2,8,4096]{3,2,1,0:T(8,128)(2,1)S(1)} async-done(((bf16[8,2,8,4096]{3,2,1,0:T(8,128)(2,1)}), bf16[8,2,8,4096]{3,2,1,0:T(8,128)(2,1)S(1)}, u32[]{:S(2)}, u32[]{:S(2)}) %all-to-all-start) | async-done | bytes 1048608 | tf_op jit(solution)/shard_map/all_to_all | solution.py:78
  53.3 1.6 copy.17
  54.9 0.0 all-gather.2.cloned.1.call-update
  54.9 0.0 all-reduce.3.cloned.1.call-start
  55.0 0.6 dynamic_slice.10
  56.2 0.0 collective-permute-done
  56.2 9.1 %constant_dynamic-update-slice_fusion = (bf16[2,3,4096,256]{3,2,1,0:T(8,128)(2,1)}, bf16[1,3,4096,256]{3,2,1,0:T(8,128)(2,1)}) fusion(bf16[2,3,4096,256]{3,2,1,0:T(8,128)(2,1)} %copy.29, s32[]{:T(128)S(6)} %select_n.80, bf16[1,3,4096,256]{3,2,1,0:T(8,128)(2,1)} %collective-permute-done, bf16[1,3,4096,256]{3,2,1,0:T(8,128)(2,1)} %constant_dynamic-slice_fusion.1, ...), kind=kLoop, calls=%fused_computation.46 | loop fusion | flops 3145728 | bytes 25166340 | tf_op jit(solution)/shard_map/dynamic_update_slice | solution.py:74
  65.3 41.4 %all-gather.2.cloned.1.call-done = bf16[32,2,8,4096]{3,0,2,1:T(8,128)(2,1)} async-done(((bf16[8,2,8,4096]{3,0,2,1:T(8,128)(2,1)}), bf16[32,2,8,4096]{3,0,2,1:T(8,128)(2,1)}) %all-gather.2.cloned.1.call-update) | async-done | bytes 4194320 | tf_op jit(solution)/shard_map/all_gather | solution.py:79
  106.7 6.9 %fusion.3 = f32[32,2,8,2,256]{4,0,2,3,1:T(8,128)S(1)} fusion(bf16[32,2,8,4096]{3,0,2,1:T(8,128)(2,1)} %all-gather.2.cloned.1.call-done, bf16[2,3,4096,256]{3,2,1,0:T(8,128)(2,1)} %get-tuple-element.8), kind=kOutput, calls=%fused_computation.9 | convolution fusion | flops 2147483648 | bytes 13631488 | tf_op jit(solution)/shard_map/ajcd,jkdh->ajckh/dot_general | solution.py:52
  113.6 0.0 copy-start.6
  113.6 5.5 %fusion.1 = bf16[32,2,8,4096]{3,0,2,1:T(8,128)(2,1)} fusion(bf16[2,3,4096,256]{3,2,1,0:T(8,128)(2,1)} %get-tuple-element.8, f32[32,2,8,2,256]{4,0,2,3,1:T(8,128)S(1)} %fusion.3), kind=kOutput, calls=%fused_computation.5 | convolution fusion | flops 1076625408 | bytes 9437184 | tf_op jit(solution)/shard_map/ajch,jdh->ajcd/dot_general | solution.py:56
  119.0 0.0 all-reduce.3.cloned.1.call-update
  119.1 0.0 copy-start.1
  119.1 0.6 dynamic-slice
  120.3 102.7 %all-reduce.3.cloned.1.call-done = bf16[32,2,8,4096]{3,0,2,1:T(8,128)(2,1)} async-done(((bf16[32,2,8,4096]{3,0,2,1:T(8,128)(2,1)}), bf16[32,2,8,4096]{3,0,2,1:T(8,128)(2,1)}) %all-reduce.3.cloned.1.call-update) | async-done | bytes 4194320
  223.1 1.3 constant_dynamic-slice_fusion
  224.4 1.6 copy.19
  225.9 4.6 %all-to-all-start.1 = ((bf16[8,2,8,4096]{3,2,1,0:T(8,128)(2,1)}), bf16[8,2,8,4096]{3,2,1,0:T(8,128)(2,1)S(1)}, u32[]{:S(2)}, u32[]{:S(2)}) async-start(bf16[8,2,8,4096]{3,2,1,0:T(8,128)(2,1)} %copy.19), calls=%async_computation.1 | async-start | bytes 2097152 | tf_op jit(solution)/shard_map/all_to_all | solution.py:81
  230.6 26.6 %all-to-all-done.1 = bf16[8,2,8,4096]{3,2,1,0:T(8,128)(2,1)S(1)} async-done(((bf16[8,2,8,4096]{3,2,1,0:T(8,128)(2,1)}), bf16[8,2,8,4096]{3,2,1,0:T(8,128)(2,1)S(1)}, u32[]{:S(2)}, u32[]{:S(2)}) %all-to-all-start.1) | async-done | bytes 1048608 | tf_op jit(solution)/shard_map/all_to_all | solution.py:81
  257.1 0.9 gather_fusion
  258.0 1.1 multiply_reduce_fusion
  (12 shorter events, 0.1 us)
Async XLA Ops:
  7.2 11.7 %copy-start = (bf16[8,4096]{1,0:T(8,128)(2,1)S(1)}, bf16[8,4096]{1,0:T(8,128)(2,1)}, u32[]{:S(2)}) copy-start(bf16[8,4096]{1,0:T(8,128)(2,1)} %param.7) | copy-start | bytes 196612
  7.2 11.0 %copy-start.2 = (s32[8,8]{1,0:T(8,128)S(1)}, s32[8,8]{1,0:T(8,128)}, u32[]{:S(2)}) copy-start(s32[8,8]{1,0:T(8,128)} %param.9) | copy-start | bytes 772
  7.2 10.9 %copy-start.5 = (s32[16]{0:T(128)S(1)}, s32[16]{0:T(128)}, u32[]{:S(2)}) copy-start(s32[16]{0:T(128)} %param.10) | copy-start | bytes 196
  7.2 10.5 %copy-start.3 = (s32[8]{0:T(128)S(1)}, s32[8]{0:T(128)}, u32[]{:S(2)}) copy-start(s32[8]{0:T(128)} %param.11) | copy-start | bytes 100
  7.2 11.2 %copy-start.4 = (s32[8]{0:T(128)S(1)}, s32[8]{0:T(128)}, u32[]{:S(2)}) copy-start(s32[8]{0:T(128)} %param.12) | copy-start | bytes 100
  20.4 32.9 %all-to-all-start = ((bf16[8,2,8,4096]{3,2,1,0:T(8,128)(2,1)}), bf16[8,2,8,4096]{3,2,1,0:T(8,128)(2,1)S(1)}, u32[]{:S(2)}, u32[]{:S(2)}) async-start(bf16[8,2,8,4096]{3,2,1,0:T(8,128)(2,1)} %bitcast.7), calls=%async_computation | async-start | bytes 2097152 | tf_op jit(solution)/shard_map/all_to_all | solution.py:78
  26.7 80.0 %all-gather.2.cloned.1.call-start = ((), (), s32[]{:S(2)}) async-start(), calls=%async_computation.2 | async-start | bytes 5242880 | tf_op jit(solution)/shard_map/all_gather | solution.py:79
  35.2 21.0 %collective-permute-start = (bf16[1,3,4096,256]{3,2,1,0:T(8,128)(2,1)}, bf16[1,3,4096,256]{3,2,1,0:T(8,128)(2,1)}, u32[]{:S(2)}, u32[]{:S(2)}) collective-permute-start(bf16[1,3,4096,256]{3,2,1,0:T(8,128)(2,1)} %constant_dynamic-slice_fusion.1), channel_id=1, source_target_pairs={{0,1},{1,0},{2,3},{3,2},{4,5},{5,4},{6,7},{7,6},{8,9},{9,8},{10,11... | collective-permute-start | bytes 18874376 | tf_op jit(solution)/shard_map/ppermute | solution.py:10
  54.9 168.2 %all-reduce.3.cloned.1.call-start = ((), (), s32[]{:S(2)}) async-start(), calls=%async_computation.3 | async-start | bytes 8388608
  113.6 5.5 %copy-start.6 = (u32[32]{0:T(128)S(1)}, u32[32]{0:T(128)}, u32[]{:S(2)}) copy-start(u32[32]{0:T(128)} %constant.94) | copy-start | bytes 388
  119.1 138.9 %copy-start.1 = (f32[8,8]{1,0:T(8,128)S(1)}, f32[8,8]{1,0:T(8,128)}, u32[]{:S(2)}) copy-start(f32[8,8]{1,0:T(8,128)} %param.8) | copy-start | bytes 772
  225.9 31.2 %all-to-all-start.1 = ((bf16[8,2,8,4096]{3,2,1,0:T(8,128)(2,1)}), bf16[8,2,8,4096]{3,2,1,0:T(8,128)(2,1)S(1)}, u32[]{:S(2)}, u32[]{:S(2)}) async-start(bf16[8,2,8,4096]{3,2,1,0:T(8,128)(2,1)} %copy.19), calls=%async_computation.1 | async-start | bytes 2097152 | tf_op jit(solution)/shard_map/all_to_all | solution.py:81
Sparse Core Ops, SparseCore 0:
  55.0 51.5 all-gather.1
  119.2 103.8 all-reduce.2
where the time goes:
time: 266 us
  waiting for transfers between devices  188 us (71%)
  local copies, waits for them, and re-layouts  23.9 us (9%)
  between operations  17.5 us (7%)
  matrix products  13.8 us (5%)
  starting transfers between devices  11.5 us (4%)
  other arithmetic  10.9 us (4%)
    unnamed x3, waiting for transfers between devices  103 us
    all_gather x1, waiting for transfers between devices, body(): lax.all_gather(arrived, 'dp', axis=0, tiled=True)  41.4 us
    all_to_all x1, waiting for transfers between devices, body(): lax.all_to_all(summed, 'expert', split_axis=0, concat_axis=0, tiled=True)  26.6 us
    all_to_all x1, waiting for transfers between devices, body(): lax.all_to_all(outgoing, 'expert', split_axis=0, concat_axis=0, tiled=True)  17.7 us
    unnamed x17, local copies, waits for them, and re-layouts  12.4 us
    dynamic_update_slice x1, other arithmetic, body(): lax.dynamic_update_slice_in_dim(expert_weights, received, moving, 0)  9.08 us
    dot_general x1, matrix products, expert_partial(): jnp.einsum('ajcd,jkdh->ajckh', row_data, weights[:, :2], preferred_elemen...  6.89 us
    all_to_all x1, starting transfers between devices, body(): lax.all_to_all(outgoing, 'expert', split_axis=0, concat_axis=0, tiled=True)  6.33 us
  transfers between devices with their start and end apart: 5, of which 4 were waited for; matrix products, arithmetic and copies ran while one was open for 7% of the time, Pallas kernels for 0%

commit v1 on v0

v1 whole, which is shorter than its diff:
```python
import functools

import jax
import jax.numpy as jnp
from jax import lax
from jax.experimental import pallas as pl
from jax.experimental.pallas import tpu as pltpu
from jax.sharding import PartitionSpec as P

MESH = pl.DeviceIdType.MESH
LANES = 128
VMEM_LIMIT = 56 * 1024 * 1024


def place(nd, nz):
    d = lax.axis_index("dp")
    e = lax.axis_index("expert")
    return d, e // 2, e % 2, e


def enter(nd, nz, d, zz, c, e):
    barrier = pltpu.get_barrier_semaphore()
    peers = [(d, zz * 2 + 1 - c)]
    peers += [(lax.rem(d + k, nd), e) for k in range(1, nd)]
    peers += [(d, lax.rem(zz + i, nz) * 2 + c) for i in range(1, nz)]
    for pd, pe in peers:
        pl.semaphore_signal(barrier, inc=1, device_id={"dp": pd, "expert": pe}, device_id_type=MESH)
    pl.semaphore_wait(barrier, len(peers))


def remote(src, dst, send, recv, pd, pe):
    return pltpu.make_async_remote_copy(
        src_ref=src,
        dst_ref=dst,
        send_sem=send,
        recv_sem=recv,
        device_id={"dp": pd, "expert": pe},
        device_id_type=MESH,
    )


def gather_kernel(
    nd, nz, mv_ref, msg_ref, w_hbm, g_ref, got_hbm,
    out_ref, w_sem, a_send, a_recv, b_send, b_recv, c_send, c_recv, s_send, s_recv, *w_refs,
):
    d, zz, c, e = place(nd, nz)
    sibling = zz * 2 + 1 - c
    slots, parts, rows, _ = w_hbm.shape
    loads = [
        [pltpu.make_async_copy(w_hbm.at[j, m], w_refs[m].at[j], w_sem.at[j, m]) for j in range(slots)]
        for m in range(parts)
    ]
    for part in loads:
        for load in part:
            load.start()
    g_ref[c, zz, d] = msg_ref[...]
    enter(nd, nz, d, zz, c, e)
    started = []
    for i in range(1, nz):
        block = g_ref.at[c, zz, d]
        copy = remote(block, block, a_send.at[i - 1], a_recv.at[i - 1], d, lax.rem(zz + i, nz) * 2 + c)
        copy.start()
        started.append(copy)

    def to_dp(i):
        block = g_ref.at[c, lax.rem(zz - i + nz, nz), d]
        for k in range(1, nd):
            copy = remote(block, block, b_send.at[i, k - 1], b_recv.at[i, k - 1], lax.rem(d + k, nd), e)
            copy.start()
            started.append(copy)

    to_dp(0)
    moving = mv_ref[0]
    tile = min(rows, 256)

    def swap(m):
        for load in loads[m]:
            load.wait()

        def step(r, carry):
            at = pl.ds(pl.multiple_of(r * tile, tile), tile)
            out_ref[m, at, :] = w_refs[m][moving, at, :]
            return carry

        lax.fori_loop(0, rows // tile, step, 0)
        copy = remote(out_ref.at[m], got_hbm.at[m], s_send.at[m], s_recv.at[m], d, sibling)
        copy.start()
        started.append(copy)
        return copy

    swaps = [swap(0)]
    for i in range(1, nz):
        block = g_ref.at[c, lax.rem(zz - i + nz, nz), d]
        remote(block, block, a_send.at[i - 1], a_recv.at[i - 1], d, e).wait_recv()
        to_dp(i)
    for m in range(1, parts):
        swaps.append(swap(m))
    groups = []
    for i in range(nz):
        at = lax.rem(zz - i + nz, nz)
        for k in range(1, nd):
            block = g_ref.at[c, at, lax.rem(d - k + nd, nd)]
            remote(block, block, b_send.at[i, k - 1], b_recv.at[i, k - 1], d, e).wait_recv()
        copy = remote(g_ref.at[c, at], g_ref.at[c, at], c_send.at[i], c_recv.at[i], d, sibling)
        copy.start()
        started.append(copy)
        groups.append(copy)
    for copy in groups + swaps:
        copy.wait_recv()
    for copy in started:
        copy.wait_send()


def expert_kernel(flag_ref, g_ref, w_hbm, got_hbm, p_ref, moved_hbm, w_ref, x_ref, h_ref, w_sem, m_sem):
    blocks, rows_of, _ = g_ref.shape
    slots, parts, width, hidden = w_hbm.shape
    lanes = (g_ref.shape[2] - width) // 2
    chunk = min(width, 1024)
    chunks = width // chunk
    e = lax.axis_index("expert")

    def load(j, m, q):
        at = pl.ds(q * chunk, chunk)
        return pltpu.make_async_copy(w_hbm.at[j, m, at], w_ref.at[j, m, at], w_sem.at[j, m, q])

    order = [(j, m, q) for j in range(slots) for q in range(chunks) for m in (0, 1)]
    order += [(j, 2, q) for q in range(chunks) for j in range(slots)]
    for key in order:
        load(*key).start()
    swapping = flag_ref[0] != 0

    @pl.when(swapping)
    def _():
        pltpu.make_async_copy(got_hbm, moved_hbm.at[0], m_sem).start()

    @pl.when(jnp.logical_not(swapping))
    def _():
        pltpu.make_async_copy(w_hbm.at[flag_ref[1]], moved_hbm.at[0], m_sem).start()

    per = min(blocks, max(1, 256 // rows_of))
    rows = per * rows_of

    def tile(t, waiting):
        at = pl.ds(t * per, per)
        x_ref[...] = g_ref[at, :, :width].astype(jnp.float32).reshape(rows, width).astype(jnp.bfloat16)
        share = (
            g_ref[at, :, width : width + lanes].astype(jnp.float32)
            + g_ref[at, :, width + lanes :].astype(jnp.float32)
        ).reshape(rows, lanes)
        lane = lax.broadcasted_iota(jnp.int32, (rows, lanes), 1)
        for j in range(slots):
            weight = jnp.sum(jnp.where(lane == e * slots + j, share, 0.0), axis=1, keepdims=True)
            gate = jnp.zeros((rows, hidden), jnp.float32)
            up = jnp.zeros((rows, hidden), jnp.float32)
            for q in range(chunks):
                cut = pl.ds(q * chunk, chunk)
                if waiting:
                    load(j, 0, q).wait()
                    load(j, 1, q).wait()
                x = x_ref[:, cut]
                gate += jnp.dot(x, w_ref[j, 0, cut, :], preferred_element_type=jnp.float32)
                up += jnp.dot(x, w_ref[j, 1, cut, :], preferred_element_type=jnp.float32)
            value = weight * (gate / (1.0 + jnp.exp(-gate)) * up)
            h_ref[:, pl.ds(j * hidden, hidden)] = value.astype(jnp.bfloat16)
        for q in range(chunks):
            cut = pl.ds(q * chunk, chunk)
            total = jnp.zeros((rows, chunk), jnp.float32)
            for j in range(slots):
                if waiting:
                    load(j, 2, q).wait()
                total += lax.dot_general(
                    h_ref[:, pl.ds(j * hidden, hidden)],
                    w_ref[j, 2, cut, :],
                    (((1,), (1,)), ((), ())),
                    preferred_element_type=jnp.float32,
                )
            p_ref[at, :, cut] = total.reshape(per, rows_of, chunk).astype(jnp.bfloat16)

    tile(0, True)
    if blocks > per:
        def step(t, carry):
            tile(t, False)
            return carry

        lax.fori_loop(1, blocks // per, step, 0)
    pltpu.make_async_copy(got_hbm, moved_hbm.at[0], m_sem).wait()


def scatter_kernel(
    nd, nz, p_ref, y_ref, rc_ref, s1_ref, rb_ref, s2_ref, ra_ref,
    a_send, a_recv, b_send, b_recv, c_send, c_recv,
):
    d, zz, c, e = place(nd, nz)
    sibling = zz * 2 + 1 - c
    f32 = jnp.float32
    enter(nd, nz, d, zz, c, e)
    started = []
    order = list(range(1, nz)) + [0]
    for i in order:
        at = lax.rem(zz + i, nz)
        copy = remote(p_ref.at[1 - c, at], rc_ref.at[i], c_send.at[i], c_recv.at[i], d, sibling)
        copy.start()
        started.append(copy)
    for i in order:
        at = lax.rem(zz + i, nz)
        remote(p_ref.at[1 - c, at], rc_ref.at[i], c_send.at[i], c_recv.at[i], d, sibling).wait_recv()
        for k in list(range(1, nd)) + [0]:
            pd = lax.rem(d + k, nd)
            s1_ref[i, k] = (p_ref[c, at, pd].astype(f32) + rc_ref[i, pd].astype(f32)).astype(jnp.bfloat16)
            if k:
                copy = remote(s1_ref.at[i, k], rb_ref.at[i, k - 1], b_send.at[i, k - 1], b_recv.at[i, k - 1], pd, e)
                copy.start()
                started.append(copy)
    final = None
    for i in order:
        total = s1_ref[i, 0].astype(f32)
        for k in range(1, nd):
            remote(s1_ref.at[i, k], rb_ref.at[i, k - 1], b_send.at[i, k - 1], b_recv.at[i, k - 1], d, e).wait_recv()
            total += rb_ref[i, k - 1].astype(f32)
        if i:
            s2_ref[i - 1] = total.astype(jnp.bfloat16)
            pe = lax.rem(zz + i, nz) * 2 + c
            copy = remote(s2_ref.at[i - 1], ra_ref.at[i - 1], a_send.at[i - 1], a_recv.at[i - 1], d, pe)
            copy.start()
            started.append(copy)
        else:
            final = total
    for i in range(1, nz):
        remote(s2_ref.at[i - 1], ra_ref.at[i - 1], a_send.at[i - 1], a_recv.at[i - 1], d, e).wait_recv()
        final += ra_ref[i - 1].astype(f32)
    y_ref[...] = final.astype(jnp.bfloat16)
    for copy in started:
        copy.wait_send()


def message(tokens, route_weight, expert_ids, placement):
    experts = placement.shape[0]
    lanes = -(-experts // LANES) * LANES
    names = jnp.arange(experts, dtype=jnp.int32)
    chosen = jnp.sum(
        jnp.where(expert_ids[:, :, None] == names[None, None, :], route_weight[:, :, None], 0.0), axis=1
    )
    slots = jnp.arange(lanes, dtype=jnp.int32)
    share = jnp.sum(
        jnp.where(placement[None, :, None] == slots[None, None, :], chosen[:, :, None], 0.0), axis=1
    )
    high = lax.reduce_precision(share, 8, 7)
    low = share - high
    return jnp.concatenate([tokens, high.astype(jnp.bfloat16), low.astype(jnp.bfloat16)], axis=1)


def body(tokens, route_weight, expert_ids, placement, pair_step, move_slot, expert_weights):
    nd = lax.axis_size("dp")
    nz = lax.axis_size("expert") // 2
    e = lax.axis_index("expert")
    rows, width = tokens.shape
    slots, parts, _, hidden = expert_weights.shape
    bf16 = jnp.bfloat16
    vmem = pl.BlockSpec(memory_space=pltpu.VMEM)
    smem = pl.BlockSpec(memory_space=pltpu.SMEM)
    anywhere = pl.BlockSpec(memory_space=pl.ANY)
    dma = pltpu.SemaphoreType.DMA

    steps = pair_step.reshape(-1, 2).sum(axis=1)
    swap_here = (lax.dynamic_index_in_dim(steps, e // 2, 0, keepdims=False) > 0).astype(jnp.int32)
    moving = lax.dynamic_index_in_dim(move_slot, e, 0, keepdims=False)
    flags = jnp.stack([swap_here, moving])
    msg = message(tokens, route_weight, expert_ids, placement)
    full = msg.shape[1]

    gathered, got = pl.pallas_call(
        functools.partial(gather_kernel, nd, nz),
        out_shape=(
            jax.ShapeDtypeStruct((2, nz, nd, rows, full), bf16),
            jax.ShapeDtypeStruct((parts, width, hidden), bf16),
        ),
        in_specs=[smem, vmem, anywhere],
        out_specs=(vmem, anywhere),
        scratch_shapes=[
            pltpu.VMEM((parts, width, hidden), bf16),
            dma((slots, parts)),
            dma((nz - 1,)), dma((nz - 1,)),
            dma((nz, nd - 1)), dma((nz, nd - 1)),
            dma((nz,)), dma((nz,)),
            dma((parts,)), dma((parts,)),
        ] + [pltpu.VMEM((slots, width, hidden), bf16)] * parts,
        compiler_params=pltpu.CompilerParams(
            collective_id=0, has_side_effects=True, vmem_limit_bytes=VMEM_LIMIT
        ),
        name="gather",
    )(moving[None], msg, expert_weights)

    blocks = 2 * nz * nd
    per = min(blocks, max(1, 256 // rows))
    chunks = width // min(width, 1024)
    partial, moved = pl.pallas_call(
        expert_kernel,
        out_shape=(
            jax.ShapeDtypeStruct((blocks, rows, width), bf16),
            jax.ShapeDtypeStruct((1, parts, width, hidden), bf16),
        ),
        in_specs=[smem, vmem, anywhere, anywhere],
        out_specs=(vmem, anywhere),
        scratch_shapes=[
            pltpu.VMEM((slots, parts, width, hidden), bf16),
            pltpu.VMEM((per * rows, width), bf16),
            pltpu.VMEM((per * rows, slots * hidden), bf16),
            dma((slots, parts, chunks)),
            dma,
        ],
        compiler_params=pltpu.CompilerParams(vmem_limit_bytes=VMEM_LIMIT),
        name="experts",
    )(flags, gathered.reshape(blocks, rows, full), expert_weights, got)

    mixed = pl.pallas_call(
        functools.partial(scatter_kernel, nd, nz),
        out_shape=jax.ShapeDtypeStruct((rows, width), bf16),
        in_specs=[vmem],
        out_specs=vmem,
        scratch_shapes=[
            pltpu.VMEM((nz, nd, rows, width), bf16),
            pltpu.VMEM((nz, nd, rows, width), bf16),
            pltpu.VMEM((nz, nd - 1, rows, width), bf16),
            pltpu.VMEM((nz - 1, rows, width), bf16),
            pltpu.VMEM((nz - 1, rows, width), bf16),
            dma((nz - 1,)), dma((nz - 1,)),
            dma((nz, nd - 1)), dma((nz, nd - 1)),
            dma((nz,)), dma((nz,)),
        ],
        compiler_params=pltpu.CompilerParams(
            collective_id=1, has_side_effects=True, vmem_limit_bytes=VMEM_LIMIT
        ),
        name="scatter",
    )(partial.reshape(2, nz, nd, rows, width))
    return mixed, moved


def solution(mesh):
    in_specs = (
        P(("dp", "expert"), None),
        P(("dp", "expert"), None),
        P(("dp", "expert"), None),
        P(),
        P(),
        P(),
        P("expert", None, None, "dp"),
    )
    out_specs = (P(("dp", "expert"), None), P("expert", None, None, "dp"))
    return jax.shard_map(body, mesh=mesh, in_specs=in_specs, out_specs=out_specs, check_vma=False)
```

time: 266 us -> 250 us (0.940)
  Pallas kernels: 0 us -> 239 us
  waiting for transfers between devices: 188 us -> 0 us
  local copies, waits for them, and re-layouts: 23.9 us -> 4.04 us
  between operations: 17.5 us -> 1.35 us
  matrix products: 13.8 us -> 0 us
  starting transfers between devices: 11.5 us -> 0 us
  other arithmetic: 10.9 us -> 4.53 us
    pallas_call x0 -> x3, Pallas kernels: none -> 239 us  [the longest x1 195 us: body(): pl.pallas_call(expert_kernel, out_shape=(jax.ShapeDtypeStruct((blocks, ro...]
    unnamed x3 -> x0, waiting for transfers between devices: 103 us -> none
    all_to_all x2 -> x0, waiting for transfers between devices: 44.2 us -> none  [the longest x1 26.6 us: body(): lax.all_to_all(summed, 'expert', split_axis=0, concat_axis=0, tiled=True)]
    all_gather x1 -> x0, waiting for transfers between devices: 41.4 us -> none  [body(): lax.all_gather(arrived, 'dp', axis=0, tiled=True)]
    dot_general x3 -> x0, matrix products: 13.8 us -> none  [the longest x1 6.89 us: expert_partial(): jnp.einsum('ajcd,jkdh->ajckh', row_data, weights[:, :2], preferred_elemen...]
    all_to_all x2 -> x0, starting transfers between devices: 10.9 us -> none  [the longest x1 6.33 us: body(): lax.all_to_all(outgoing, 'expert', split_axis=0, concat_axis=0, tiled=True)]
    unnamed x17 -> x1, local copies, waits for them, and re-layouts: 12.4 us -> 1.47 us
    dynamic_update_slice x1 -> x0, other arithmetic: 9.08 us -> none  [body(): lax.dynamic_update_slice_in_dim(expert_weights, received, moving, 0)]
  transfers between devices with their start and end apart: 5 -> 0, of which waited for: 4 -> 0; matrix products, arithmetic and copies ran while one was open for 7% -> 0% of each run, Pallas kernels for 0% -> 0%
where the time goes in v1:
time: 250 us; the launch traced here: 249 us
  Pallas kernels  239 us (96%)
  other arithmetic  4.53 us (2%)
  local copies, waits for them, and re-layouts  4.04 us (2%)
    pallas_call x1, Pallas kernels, body(): pl.pallas_call(expert_kernel, out_shape=(jax.ShapeDtypeStruct((blocks, ro...  195 us
    pallas_call x1, Pallas kernels, body(): pl.pallas_call(functools.partial(gather_kernel, nd, nz), out_shape=(jax.S...  24.1 us
    pallas_call x1, Pallas kernels, body(): pl.pallas_call(functools.partial(scatter_kernel, nd, nz), out_shape=jax.S...  20.4 us

profile of v1, /device:TPU:0, one launch (start us, length us, event | category | flops | bytes accessed | tf_op | source)
XLA Modules:
  0.0 249.3 jit_solution(6436043241271479329)
XLA Ops:
  0.6 1.2 dynamic_slice.9.mv_ref
  1.9 0.7 iota_compare_fusion.1
  2.6 0.7 reshape.42
  3.4 0.1 reduce_sum.27
  3.5 0.6 dynamic_slice.8
  4.7 1.3 pad_add_fusion.flag_ref
  6.0 0.8 select_reduce_fusion.1
  6.8 0.1 select_reduce_fusion
  6.9 1.5 pad_maximum_fusion.msg_ref
  8.4 24.1 %gather.1 = (bf16[2,4,4,8,4352]{4,3,2,1,0:T(8,128)(2,1)}, bf16[3,4096,256]{2,1,0:T(8,128)(2,1)}) custom-call(s32[1]{0:T(128)} %dynamic_slice.9.mv_ref, bf16[8,4352]{1,0:T(8,128)(2,1)} %pad_maximum_fusion.msg_ref, bf16[2,3,4096,256]{3,2,1,0:T(8,128)(2,1)} %w_hbm.3), custom_call_target="tpu_custom_call" | custom-call | tf_op jit(solution)/shard_map/gather/pallas_call | solution.py:271
  32.5 194.9 %experts.1 = (bf16[32,8,4096]{2,1,0:T(8,128)(2,1)}, bf16[1,3,4096,256]{3,2,1,0:T(8,128)(2,1)}) custom-call(s32[2]{0:T(128)} %pad_add_fusion.flag_ref, bf16[32,8,4352]{2,1,0:T(8,128)(2,1)} %bitcast.2, bf16[2,3,4096,256]{3,2,1,0:T(8,128)(2,1)} %w_hbm.3, bf16[3,4096,256]{2,1,0:T(8,128)(2,1)} %get-tuple-element.7.got_hbm), custom_call_target="tpu_custom_call" | custom-call | tf_op jit(solution)/shard_map/experts/pallas_call | solution.py:296
  227.5 20.4 %scatter.1 = bf16[8,4096]{1,0:T(8,128)(2,1)} custom-call(bf16[2,4,4,8,4096]{4,3,2,1,0:T(8,128)(2,1)} %bitcast.3), custom_call_target="tpu_custom_call" | custom-call | tf_op jit(solution)/shard_map/scatter/pallas_call | solution.py:315
  247.9 1.5 copy.10
  (1 shorter events, 0.0 us)

commit v2 on v1

--- a/solution.py
+++ b/solution.py
@@ -40,7 +40,7 @@
 
 
 def gather_kernel(
-    nd, nz, mv_ref, msg_ref, w_hbm, g_ref, got_hbm,
+    nd, nz, mv_ref, x_ref, rw_ref, id_ref, w_hbm, g_ref, got_hbm,
     out_ref, w_sem, a_send, a_recv, b_send, b_recv, c_send, c_recv, s_send, s_recv, *w_refs,
 ):
     d, zz, c, e = place(nd, nz)
@@ -53,7 +53,16 @@
     for part in loads:
         for load in part:
             load.start()
-    g_ref[c, zz, d] = msg_ref[...]
+    width = x_ref.shape[1]
+    lanes = (g_ref.shape[4] - width) // 2
+    lane = lax.broadcasted_iota(jnp.int32, (x_ref.shape[0], lanes), 1)
+    share = jnp.zeros(lane.shape, jnp.float32)
+    for k in range(id_ref.shape[1]):
+        share += jnp.where(lane == id_ref[:, k : k + 1], rw_ref[:, k : k + 1], 0.0)
+    high = share.astype(jnp.bfloat16)
+    g_ref[c, zz, d, :, :width] = x_ref[...]
+    g_ref[c, zz, d, :, width : width + lanes] = high
+    g_ref[c, zz, d, :, width + lanes :] = (share - high.astype(jnp.float32)).astype(jnp.bfloat16)
     enter(nd, nz, d, zz, c, e)
     started = []
     for i in range(1, nz):
@@ -70,7 +79,7 @@
             started.append(copy)
 
     to_dp(0)
-    moving = mv_ref[0]
+    moving = mv_ref[e]
     tile = min(rows, 256)
 
     def swap(m):
@@ -111,7 +120,10 @@
         copy.wait_send()
 
 
-def expert_kernel(flag_ref, g_ref, w_hbm, got_hbm, p_ref, moved_hbm, w_ref, x_ref, h_ref, w_sem, m_sem):
+def expert_kernel(
+    place_ref, step_ref, mv_ref, g_ref, w_hbm, got_hbm, p_ref, moved_hbm,
+    w_ref, x_ref, h_ref, m_ref, w_sem, m_sem, o_sem,
+):
     blocks, rows_of, _ = g_ref.shape
     slots, parts, width, hidden = w_hbm.shape
     lanes = (g_ref.shape[2] - width) // 2
@@ -127,15 +139,26 @@
     order += [(j, 2, q) for q in range(chunks) for j in range(slots)]
     for key in order:
         load(*key).start()
-    swapping = flag_ref[0] != 0
+    first = e // 2 * 2
+    swapping = step_ref[first] + step_ref[first + 1] > 0
 
     @pl.when(swapping)
     def _():
-        pltpu.make_async_copy(got_hbm, moved_hbm.at[0], m_sem).start()
+        for m in range(parts):
+            pltpu.make_async_copy(got_hbm.at[m], m_ref.at[m], m_sem.at[m]).start()
 
     @pl.when(jnp.logical_not(swapping))
     def _():
-        pltpu.make_async_copy(w_hbm.at[flag_ref[1]], moved_hbm.at[0], m_sem).start()
+        for m in range(parts):
+            pltpu.make_async_copy(w_hbm.at[mv_ref[e], m], m_ref.at[m], m_sem.at[m]).start()
+
+    def put(m):
+        return pltpu.make_async_copy(m_ref.at[m], moved_hbm.at[0, m], o_sem.at[m])
+
+    def put_all():
+        for m in range(parts):
+            pltpu.make_async_copy(got_hbm.at[m], m_ref.at[m], m_sem.at[m]).wait()
+            put(m).start()
 
     per = min(blocks, max(1, 256 // rows_of))
     rows = per * rows_of
@@ -147,9 +170,12 @@
             g_ref[at, :, width : width + lanes].astype(jnp.float32)
             + g_ref[at, :, width + lanes :].astype(jnp.float32)
         ).reshape(rows, lanes)
-        lane = lax.broadcasted_iota(jnp.int32, (rows, lanes), 1)
+        lane = lax.broadcasted_iota(jnp.int32, (1, lanes), 1)
+        held = jnp.full((1, lanes), -1, jnp.int32)
+        for name in range(place_ref.shape[0]):
+            held = jnp.where(lane == name, place_ref[name], held)
         for j in range(slots):
-            weight = jnp.sum(jnp.where(lane == e * slots + j, share, 0.0), axis=1, keepdims=True)
+            weight = jnp.sum(jnp.where(held == e * slots + j, share, 0.0), axis=1, keepdims=True)
             gate = jnp.zeros((rows, hidden), jnp.float32)
             up = jnp.zeros((rows, hidden), jnp.float32)
             for q in range(chunks):
@@ -163,6 +189,8 @@
             value = weight * (gate / (1.0 + jnp.exp(-gate)) * up)
             h_ref[:, pl.ds(j * hidden, hidden)] = value.astype(jnp.bfloat16)
         for q in range(chunks):
+            if waiting and q == chunks // 2:
+                put_all()
             cut = pl.ds(q * chunk, chunk)
             total = jnp.zeros((rows, chunk), jnp.float32)
             for j in range(slots):
@@ -183,7 +211,8 @@
             return carry
 
         lax.fori_loop(1, blocks // per, step, 0)
-    pltpu.make_async_copy(got_hbm, moved_hbm.at[0], m_sem).wait()
+    for m in range(parts):
+        put(m).wait()
 
 
 def scatter_kernel(
@@ -233,22 +262,6 @@
         copy.wait_send()
 
 
-def message(tokens, route_weight, expert_ids, placement):
-    experts = placement.shape[0]
-    lanes = -(-experts // LANES) * LANES
-    names = jnp.arange(experts, dtype=jnp.int32)
-    chosen = jnp.sum(
-        jnp.where(expert_ids[:, :, None] == names[None, None, :], route_weight[:, :, None], 0.0), axis=1
-    )
-    slots = jnp.arange(lanes, dtype=jnp.int32)
-    share = jnp.sum(
-        jnp.where(placement[None, :, None] == slots[None, None, :], chosen[:, :, None], 0.0), axis=1
-    )
-    high = lax.reduce_precision(share, 8, 7)
-    low = share - high
-    return jnp.concatenate([tokens, high.astype(jnp.bfloat16), low.astype(jnp.bfloat16)], axis=1)
-
-
 def body(tokens, route_weight, expert_ids, placement, pair_step, move_slot, expert_weights):
     nd = lax.axis_size("dp")
     nz = lax.axis_size("expert") // 2
@@ -261,12 +274,8 @@
     anywhere = pl.BlockSpec(memory_space=pl.ANY)
     dma = pltpu.SemaphoreType.DMA
 
-    steps = pair_step.reshape(-1, 2).sum(axis=1)
-    swap_here = (lax.dynamic_index_in_dim(steps, e // 2, 0, keepdims=False) > 0).astype(jnp.int32)
-    moving = lax.dynamic_index_in_dim(move_slot, e, 0, keepdims=False)
-    flags = jnp.stack([swap_here, moving])
-    msg = message(tokens, route_weight, expert_ids, placement)
-    full = msg.shape[1]
+    experts = placement.shape[0]
+    full = width + 2 * (-(-experts // LANES) * LANES)
 
     gathered, got = pl.pallas_call(
         functools.partial(gather_kernel, nd, nz),
@@ -274,7 +283,7 @@
             jax.ShapeDtypeStruct((2, nz, nd, rows, full), bf16),
             jax.ShapeDtypeStruct((parts, width, hidden), bf16),
         ),
-        in_specs=[smem, vmem, anywhere],
+        in_specs=[smem, vmem, vmem, vmem, anywhere],
         out_specs=(vmem, anywhere),
         scratch_shapes=[
             pltpu.VMEM((parts, width, hidden), bf16),
@@ -288,7 +297,7 @@
             collective_id=0, has_side_effects=True, vmem_limit_bytes=VMEM_LIMIT
         ),
         name="gather",
-    )(moving[None], msg, expert_weights)
+    )(move_slot, tokens, route_weight, expert_ids, expert_weights)
 
     blocks = 2 * nz * nd
     per = min(blocks, max(1, 256 // rows))
@@ -299,18 +308,20 @@
             jax.ShapeDtypeStruct((blocks, rows, width), bf16),
             jax.ShapeDtypeStruct((1, parts, width, hidden), bf16),
         ),
-        in_specs=[smem, vmem, anywhere, anywhere],
+        in_specs=[smem, smem, smem, vmem, anywhere, anywhere],
         out_specs=(vmem, anywhere),
         scratch_shapes=[
             pltpu.VMEM((slots, parts, width, hidden), bf16),
             pltpu.VMEM((per * rows, width), bf16),
             pltpu.VMEM((per * rows, slots * hidden), bf16),
+            pltpu.VMEM((parts, width, hidden), bf16),
             dma((slots, parts, chunks)),
-            dma,
+            dma((parts,)),
+            dma((parts,)),
         ],
         compiler_params=pltpu.CompilerParams(vmem_limit_bytes=VMEM_LIMIT),
         name="experts",
-    )(flags, gathered.reshape(blocks, rows, full), expert_weights, got)
+    )(placement, pair_step, move_slot, gathered.reshape(blocks, rows, full), expert_weights, got)
 
     mixed = pl.pallas_call(
         functools.partial(scatter_kernel, nd, nz),

time: 250 us -> 58.1 us (0.23)
  Pallas kernels: 239 us -> 55.3 us
  other arithmetic: 4.53 us -> 0 us
  local copies, waits for them, and re-layouts: 4.04 us -> 1.47 us
    pallas_call x1, Pallas kernels: 195 us -> 11.4 us  [body(): pl.pallas_call(expert_kernel, out_shape=(jax.ShapeDtypeStruct((blocks, ro...]
where the time goes in v2:
time: 58.1 us; the launch traced here: 57.4 us
  Pallas kernels  55.3 us (95%)
  local copies, waits for them, and re-layouts  1.47 us (3%)
  between operations  0.65 us (1%)
    pallas_call x1, Pallas kernels, body(): pl.pallas_call(functools.partial(gather_kernel, nd, nz), out_shape=(jax.S...  23.5 us
    pallas_call x1, Pallas kernels, body(): pl.pallas_call(functools.partial(scatter_kernel, nd, nz), out_shape=jax.S...  20.4 us
    pallas_call x1, Pallas kernels, body(): pl.pallas_call(expert_kernel, out_shape=(jax.ShapeDtypeStruct((blocks, ro...  11.4 us
    unnamed x1, local copies, waits for them, and re-layouts  1.47 us

profile of v2, /device:TPU:0, one launch (start us, length us, event | category | flops | bytes accessed | tf_op | source)
XLA Modules:
  0.0 57.4 jit_solution(5135598245358445771)
XLA Ops:
  0.6 23.5 %gather.1 = (bf16[2,4,4,8,4352]{4,3,2,1,0:T(8,128)(2,1)}, bf16[3,4096,256]{2,1,0:T(8,128)(2,1)}) custom-call(s32[8]{0:T(128)} %mv_ref.3, bf16[8,4096]{1,0:T(8,128)(2,1)} %x_ref.1, f32[8,8]{1,0:T(8,128)} %rw_ref.1, s32[8,8]{1,0:T(8,128)} %id_ref.1, bf16[2,3,4096,256]{3,2,1,0:T(8,128)(2,1)} %w_hbm.3), custom_call_target="tpu_custom_call" | custom-call | tf_op jit(solution)/shard_map/gather/pallas_call | solution.py:280
  24.1 11.4 %experts.1 = (bf16[32,8,4096]{2,1,0:T(8,128)(2,1)}, bf16[1,3,4096,256]{3,2,1,0:T(8,128)(2,1)}) custom-call(s32[16]{0:T(128)} %place_ref.1, s32[8]{0:T(128)} %step_ref.1, s32[8]{0:T(128)} %mv_ref.3, bf16[32,8,4352]{2,1,0:T(8,128)(2,1)} %bitcast.2, bf16[2,3,4096,256]{3,2,1,0:T(8,128)(2,1)} %w_hbm.3, bf16[3,4096,256]{2,1,0:T(8,128)(2,1)} %get-tuple-element.7.got_hbm), custom_call_target="tpu_custom_call" | custom-call | tf_op jit(solution)/shard_map/experts/pallas_call | solution.py:305
  35.5 20.4 %scatter.1 = bf16[8,4096]{1,0:T(8,128)(2,1)} custom-call(bf16[2,4,4,8,4096]{4,3,2,1,0:T(8,128)(2,1)} %bitcast.3), custom_call_target="tpu_custom_call" | custom-call | tf_op jit(solution)/shard_map/scatter/pallas_call | solution.py:326
  55.9 1.5 %copy.10 = bf16[8,4096]{1,0:T(8,128)(2,1)} copy(bf16[8,4096]{1,0:T(8,128)(2,1)} %scatter.1) | data formatting | bytes 131072

commit v3 on v2

--- a/solution.py
+++ b/solution.py
@@ -16,6 +16,18 @@
     d = lax.axis_index("dp")
     e = lax.axis_index("expert")
     return d, e // 2, e % 2, e
+
+
+def around(nd, d):
+    if nd == 4:
+        x, y = lax.rem(d, 2), d // 2
+        near = [y * 2 + 1 - x, (1 - y) * 2 + x, 3 - d]
+        return True, near, near
+    return (
+        False,
+        [lax.rem(d + k, nd) for k in range(1, nd)],
+        [lax.rem(d - k + nd, nd) for k in range(1, nd)],
+    )
 
 
 def enter(nd, nz, d, zz, c, e):
@@ -64,6 +76,7 @@
     g_ref[c, zz, d, :, width : width + lanes] = high
     g_ref[c, zz, d, :, width + lanes :] = (share - high.astype(jnp.float32)).astype(jnp.bfloat16)
     enter(nd, nz, d, zz, c, e)
+    square, peers, origins = around(nd, d)
     started = []
     for i in range(1, nz):
         block = g_ref.at[c, zz, d]
@@ -73,10 +86,24 @@
 
     def to_dp(i):
         block = g_ref.at[c, lax.rem(zz - i + nz, nz), d]
-        for k in range(1, nd):
-            copy = remote(block, block, b_send.at[i, k - 1], b_recv.at[i, k - 1], lax.rem(d + k, nd), e)
+        for k in range(1, 3 if square else nd):
+            copy = remote(block, block, b_send.at[i, k - 1], b_recv.at[i, k - 1], peers[k - 1], e)
             copy.start()
             started.append(copy)
+
+    def arrived(i, k):
+        block = g_ref.at[c, lax.rem(zz - i + nz, nz), origins[k - 1]]
+        remote(block, block, b_send.at[i, k - 1], b_recv.at[i, k - 1], d, e).wait_recv()
+
+    def forward(i):
+        if not square:
+            return
+        arrived(i, 1)
+        arrived(i, 2)
+        block = g_ref.at[c, lax.rem(zz - i + nz, nz), peers[i % 2]]
+        copy = remote(block, block, b_send.at[i, 2], b_recv.at[i, 2], peers[1 - i % 2], e)
+        copy.start()
+        started.append(copy)
 
     to_dp(0)
     moving = mv_ref[e]
@@ -102,14 +129,17 @@
         block = g_ref.at[c, lax.rem(zz - i + nz, nz), d]
         remote(block, block, a_send.at[i - 1], a_recv.at[i - 1], d, e).wait_recv()
         to_dp(i)
-    for m in range(1, parts):
+        forward(i - 1)
+        if i < parts:
+            swaps.append(swap(i))
+    forward(nz - 1)
+    for m in range(max(1, nz), parts):
         swaps.append(swap(m))
     groups = []
     for i in range(nz):
         at = lax.rem(zz - i + nz, nz)
-        for k in range(1, nd):
-            block = g_ref.at[c, at, lax.rem(d - k + nd, nd)]
-            remote(block, block, b_send.at[i, k - 1], b_recv.at[i, k - 1], d, e).wait_recv()
+        for k in range(3 if square else 1, nd):
+            arrived(i, k)
         copy = remote(g_ref.at[c, at], g_ref.at[c, at], c_send.at[i], c_recv.at[i], d, sibling)
         copy.start()
         started.append(copy)
@@ -230,22 +260,46 @@
         copy = remote(p_ref.at[1 - c, at], rc_ref.at[i], c_send.at[i], c_recv.at[i], d, sibling)
         copy.start()
         started.append(copy)
+    square, peers, origins = around(nd, d)
+
+    def own(i, pd):
+        return p_ref[c, lax.rem(zz + i, nz), pd].astype(f32) + rc_ref[i, pd].astype(f32)
+
+    def send(i, k, src, dst, pd):
+        copy = remote(src, dst, b_send.at[i, k], b_recv.at[i, k], pd, e)
+        copy.start()
+        started.append(copy)
+
+    def arrived(i, k, dst):
+        remote(dst, dst, b_send.at[i, k], b_recv.at[i, k], d, e).wait_recv()
+
     for i in order:
         at = lax.rem(zz + i, nz)
         remote(p_ref.at[1 - c, at], rc_ref.at[i], c_send.at[i], c_recv.at[i], d, sibling).wait_recv()
-        for k in list(range(1, nd)) + [0]:
-            pd = lax.rem(d + k, nd)
-            s1_ref[i, k] = (p_ref[c, at, pd].astype(f32) + rc_ref[i, pd].astype(f32)).astype(jnp.bfloat16)
-            if k:
-                copy = remote(s1_ref.at[i, k], rb_ref.at[i, k - 1], b_send.at[i, k - 1], b_recv.at[i, k - 1], pd, e)
-                copy.start()
-                started.append(copy)
+        if square:
+            s1_ref[i, 0] = own(i, peers[i % 2]).astype(jnp.bfloat16)
+            s1_ref[i, 1] = own(i, peers[2]).astype(jnp.bfloat16)
+            send(i, 0, s1_ref.at[i, pl.ds(0, 2)], rb_ref.at[i, pl.ds(0, 2)], peers[i % 2])
+            continue
+        for k in range(1, nd):
+            s1_ref[i, k - 1] = own(i, peers[k - 1]).astype(jnp.bfloat16)
+            send(i, k - 1, s1_ref.at[i, k - 1], rb_ref.at[i, k - 1], peers[k - 1])
+    if square:
+        for i in order:
+            arrived(i, 0, rb_ref.at[i, pl.ds(0, 2)])
+            far = peers[1 - i % 2]
+            s1_ref[i, 2] = (own(i, far) + rb_ref[i, 1].astype(f32)).astype(jnp.bfloat16)
+            send(i, 1, s1_ref.at[i, 2], rb_ref.at[i, 2], far)
     final = None
     for i in order:
-        total = s1_ref[i, 0].astype(f32)
-        for k in range(1, nd):
-            remote(s1_ref.at[i, k], rb_ref.at[i, k - 1], b_send.at[i, k - 1], b_recv.at[i, k - 1], d, e).wait_recv()
-            total += rb_ref[i, k - 1].astype(f32)
+        total = own(i, d)
+        if square:
+            arrived(i, 1, rb_ref.at[i, 2])
+            total += rb_ref[i, 0].astype(f32) + rb_ref[i, 2].astype(f32)
+        else:
+            for k in range(1, nd):
+                arrived(i, k - 1, rb_ref.at[i, k - 1])
+                total += rb_ref[i, k - 1].astype(f32)
         if i:
             s2_ref[i - 1] = total.astype(jnp.bfloat16)
             pe = lax.rem(zz + i, nz) * 2 + c
@@ -330,7 +384,7 @@
         out_specs=vmem,
         scratch_shapes=[
             pltpu.VMEM((nz, nd, rows, width), bf16),
-            pltpu.VMEM((nz, nd, rows, width), bf16),
+            pltpu.VMEM((nz, nd - 1, rows, width), bf16),
             pltpu.VMEM((nz, nd - 1, rows, width), bf16),
             pltpu.VMEM((nz - 1, rows, width), bf16),
             pltpu.VMEM((nz - 1, rows, width), bf16),

time: 58.1 us -> 63 us (1.084)
  Pallas kernels: 55.3 us -> 60.1 us
    pallas_call x1, Pallas kernels: 20.4 us -> 23.6 us  [body(): pl.pallas_call(functools.partial(scatter_kernel, nd, nz), out_shape=jax.S...]
    pallas_call x1, Pallas kernels: 23.5 us -> 25.2 us  [body(): pl.pallas_call(functools.partial(gather_kernel, nd, nz), out_shape=(jax.S...]
where the time goes in v3:
time: 63 us; the launch traced here: 62.3 us
  Pallas kernels  60.1 us (95%)
  local copies, waits for them, and re-layouts  1.47 us (2%)
  between operations  0.65 us (1%)
    pallas_call x1, Pallas kernels, body(): pl.pallas_call(functools.partial(gather_kernel, nd, nz), out_shape=(jax.S...  25.2 us
    pallas_call x1, Pallas kernels, body(): pl.pallas_call(functools.partial(scatter_kernel, nd, nz), out_shape=jax.S...  23.6 us
    pallas_call x1, Pallas kernels, body(): pl.pallas_call(expert_kernel, out_shape=(jax.ShapeDtypeStruct((blocks, ro...  11.3 us
    unnamed x1, local copies, waits for them, and re-layouts  1.47 us

profile of v3, /device:TPU:0, one launch (start us, length us, event | category | flops | bytes accessed | tf_op | source)
XLA Modules:
  0.0 62.3 jit_solution(6861109723180976016)
XLA Ops:
  0.6 25.2 %gather.1 = (bf16[2,4,4,8,4352]{4,3,2,1,0:T(8,128)(2,1)}, bf16[3,4096,256]{2,1,0:T(8,128)(2,1)}) custom-call(s32[8]{0:T(128)} %mv_ref.3, bf16[8,4096]{1,0:T(8,128)(2,1)} %x_ref.1, f32[8,8]{1,0:T(8,128)} %rw_ref.1, s32[8,8]{1,0:T(8,128)} %id_ref.1, bf16[2,3,4096,256]{3,2,1,0:T(8,128)(2,1)} %w_hbm.3), custom_call_target="tpu_custom_call" | custom-call | tf_op jit(solution)/shard_map/gather/pallas_call | solution.py:334
  25.8 11.3 %experts.1 = (bf16[32,8,4096]{2,1,0:T(8,128)(2,1)}, bf16[1,3,4096,256]{3,2,1,0:T(8,128)(2,1)}) custom-call(s32[16]{0:T(128)} %place_ref.1, s32[8]{0:T(128)} %step_ref.1, s32[8]{0:T(128)} %mv_ref.3, bf16[32,8,4352]{2,1,0:T(8,128)(2,1)} %bitcast.2, bf16[2,3,4096,256]{3,2,1,0:T(8,128)(2,1)} %w_hbm.3, bf16[3,4096,256]{2,1,0:T(8,128)(2,1)} %get-tuple-element.7.got_hbm), custom_call_target="tpu_custom_call" | custom-call | tf_op jit(solution)/shard_map/experts/pallas_call | solution.py:359
  37.2 23.6 %scatter.1 = bf16[8,4096]{1,0:T(8,128)(2,1)} custom-call(bf16[2,4,4,8,4096]{4,3,2,1,0:T(8,128)(2,1)} %bitcast.3), custom_call_target="tpu_custom_call" | custom-call | tf_op jit(solution)/shard_map/scatter/pallas_call | solution.py:380
  60.8 1.5 %copy.10 = bf16[8,4096]{1,0:T(8,128)(2,1)} copy(bf16[8,4096]{1,0:T(8,128)(2,1)} %scatter.1) | data formatting | bytes 131072

commit v4 on v0

v4 whole, which is shorter than its diff:
```python
import functools

import jax
import jax.numpy as jnp
from jax import lax
from jax.experimental import pallas as pl
from jax.experimental.pallas import tpu as pltpu
from jax.sharding import PartitionSpec as P

MESH = pl.DeviceIdType.MESH
LANES = 128
VMEM_LIMIT = 56 * 1024 * 1024


def place(nd, nz):
    d = lax.axis_index("dp")
    e = lax.axis_index("expert")
    return d, e // 2, e % 2, e


def enter(nd, nz, d, zz, c, e):
    barrier = pltpu.get_barrier_semaphore()
    peers = [(d, zz * 2 + 1 - c)]
    peers += [(lax.rem(d + k, nd), e) for k in range(1, nd)]
    peers += [(d, lax.rem(zz + i, nz) * 2 + c) for i in range(1, nz)]
    for pd, pe in peers:
        pl.semaphore_signal(barrier, inc=1, device_id={"dp": pd, "expert": pe}, device_id_type=MESH)
    pl.semaphore_wait(barrier, len(peers))


def remote(src, dst, send, recv, pd, pe):
    return pltpu.make_async_remote_copy(
        src_ref=src,
        dst_ref=dst,
        send_sem=send,
        recv_sem=recv,
        device_id={"dp": pd, "expert": pe},
        device_id_type=MESH,
    )


def layer_kernel(
    nd, nz, place_ref, step_ref, mv_ref, x_ref, rw_ref, id_ref, w_hbm, y_ref, moved_hbm,
    g_ref, t_ref, h_ref, out_ref, got_ref, rc_ref, rb_ref, s2_ref, ra_ref, *rest,
):
    d, zz, c, e = place(nd, nz)
    sibling = zz * 2 + 1 - c
    f32, bf16 = jnp.float32, jnp.bfloat16
    slots, parts, width, hidden = w_hbm.shape
    w_refs = rest[:parts]
    (w_sem, o_sem, s_send, s_recv, a_send, a_recv, b_send, b_recv, c_send, c_recv,
     ra_send, ra_recv, rb_send, rb_recv, rc_send, rc_recv) = rest[parts:]
    tokens, lanes = x_ref.shape[0], (g_ref.shape[3] - width) // 2
    loads = [
        [pltpu.make_async_copy(w_hbm.at[j, m], w_refs[m].at[j], w_sem.at[j, m]) for j in range(slots)]
        for m in range(parts)
    ]
    for part in loads:
        for load in part:
            load.start()
    lane = lax.broadcasted_iota(jnp.int32, (tokens, lanes), 1)
    share = jnp.zeros(lane.shape, f32)
    for k in range(id_ref.shape[1]):
        share += jnp.where(lane == id_ref[:, k : k + 1], rw_ref[:, k : k + 1], 0.0)
    high = share.astype(bf16)
    mine = zz * nd + d
    g_ref[c, mine, :, :width] = x_ref[...]
    g_ref[c, mine, :, width : width + lanes] = high
    g_ref[c, mine, :, width + lanes :] = (share - high.astype(f32)).astype(bf16)
    enter(nd, nz, d, zz, c, e)

    sent = []

    def send(src, dst, send_sem, recv_sem, pd, pe):
        copy = remote(src, dst, send_sem, recv_sem, pd, pe)
        copy.start()
        sent.append(copy)

    def arrived(dst, recv_sem):
        remote(dst, dst, recv_sem, recv_sem, d, sibling).wait_recv()

    def line(i):
        return lax.rem(zz - i + nz, nz)

    for i in range(1, nz):
        block = g_ref.at[c, mine]
        send(block, block, a_send.at[i - 1], a_recv.at[i - 1], d, lax.rem(zz + i, nz) * 2 + c)

    def to_dp(i):
        block = g_ref.at[c, line(i) * nd + d]
        for k in range(1, nd):
            send(block, block, b_send.at[i, k - 1], b_recv.at[i, k - 1], lax.rem(d + k, nd), e)

    to_dp(0)
    moving = mv_ref[e]
    tall = min(width, 256)
    swaps = []

    def rows_loop(fn):
        def step(r, carry):
            fn(pl.ds(pl.multiple_of(r * tall, tall), tall))
            return carry

        lax.fori_loop(0, width // tall, step, 0)

    def swap(m):
        for load in loads[m]:
            load.wait()

        def one(at):
            out_ref[m, at, :] = w_refs[m][moving, at, :]

        rows_loop(one)
        copy = remote(out_ref.at[m], got_ref.at[m], s_send.at[m], s_recv.at[m], d, sibling)
        copy.start()
        swaps.append(copy)

    swap(0)
    for i in range(1, nz):
        arrived(g_ref.at[c, line(i) * nd + d], a_recv.at[i - 1])
        to_dp(i)
    for m in range(1, parts):
        swap(m)
    for i in range(nz):
        for k in range(1, nd):
            arrived(g_ref.at[c, line(i) * nd + lax.rem(d - k + nd, nd)], b_recv.at[i, k - 1])
        group = pl.ds(line(i) * nd, nd)
        send(g_ref.at[c, group], g_ref.at[c, group], c_send.at[i], c_recv.at[i], d, sibling)

    blocks = nz * nd
    per = min(blocks, max(1, 256 // tokens))
    rows = per * tokens
    row = lax.broadcasted_iota(jnp.int32, (1, lanes), 1)
    held = jnp.full((1, lanes), -1, jnp.int32)
    for name in range(place_ref.shape[0]):
        held = jnp.where(row == name, place_ref[name], held)

    def each(fn):
        if blocks == per:
            fn(0)
            return

        def step(t, carry):
            fn(t)
            return carry

        lax.fori_loop(0, blocks // per, step, 0)

    chunk = min(width, 1024)

    def gate_up(half):
        def one(t):
            at = pl.ds(t * per, per)
            t_ref[...] = g_ref[half, at, :, :width].astype(f32).reshape(rows, width).astype(bf16)
            part = (
                g_ref[half, at, :, width : width + lanes].astype(f32)
                + g_ref[half, at, :, width + lanes :].astype(f32)
            ).reshape(rows, lanes)
            for j in range(slots):
                weight = jnp.sum(jnp.where(held == e * slots + j, part, 0.0), axis=1, keepdims=True)
                gate = jnp.zeros((rows, hidden), f32)
                up = jnp.zeros((rows, hidden), f32)
                for q in range(0, width, chunk):
                    x = t_ref[:, q : q + chunk]
                    gate += jnp.dot(x, w_refs[0][j, q : q + chunk, :], preferred_element_type=f32)
                    up += jnp.dot(x, w_refs[1][j, q : q + chunk, :], preferred_element_type=f32)
                value = weight * (gate / (1.0 + jnp.exp(-gate)) * up)
                h_ref[half, pl.ds(t * rows, rows), j * hidden : (j + 1) * hidden] = value.astype(bf16)

        each(one)

    def down(half):
        def one(t):
            at = pl.ds(t * per, per)
            for q in range(0, width, chunk):
                total = jnp.zeros((rows, chunk), f32)
                for j in range(slots):
                    total += lax.dot_general(
                        h_ref[half, pl.ds(t * rows, rows), j * hidden : (j + 1) * hidden],
                        w_refs[2][j, q : q + chunk, :],
                        (((1,), (1,)), ((), ())),
                        preferred_element_type=f32,
                    )
                g_ref[half, at, :, q : q + chunk] = total.reshape(per, tokens, chunk).astype(bf16)

        each(one)

    gate_up(c)
    for i in range(nz):
        arrived(g_ref.at[1 - c, pl.ds(line(i) * nd, nd)], c_recv.at[i])
    gate_up(1 - c)
    for copy in sent:
        copy.wait_send()
    sent.clear()
    down(1 - c)

    order = list(range(1, nz)) + [0]

    def ahead(i):
        return lax.rem(zz + i, nz)

    def p_view(half, at):
        return g_ref.at[half, pl.ds(at * nd, nd), :, pl.ds(0, width)]

    for i in order:
        send(p_view(1 - c, ahead(i)), rc_ref.at[i], rc_send.at[i], rc_recv.at[i], d, sibling)
    down(c)
    for i in order:
        arrived(rc_ref.at[i], rc_recv.at[i])
        for k in list(range(1, nd)) + [0]:
            pd = lax.rem(d + k, nd)
            rc_ref[i, pd] = (g_ref[c, ahead(i) * nd + pd, :, :width].astype(f32) + rc_ref[i, pd].astype(f32)).astype(bf16)
            if k:
                send(rc_ref.at[i, pd], rb_ref.at[i, k - 1], rb_send.at[i, k - 1], rb_recv.at[i, k - 1], pd, e)
    first = e // 2 * 2
    swapping = step_ref[first] + step_ref[first + 1] > 0
    puts = []
    for m in range(parts):
        swaps[m].wait_recv()

        def one(at):
            got_ref[m, at, :] = lax.select(swapping, got_ref[m, at, :], out_ref[m, at, :])

        rows_loop(one)
        put = pltpu.make_async_copy(got_ref.at[m], moved_hbm.at[0, m], o_sem.at[m])
        put.start()
        puts.append(put)
    final = None
    for i in order:
        total = rc_ref[i, d].astype(f32)
        for k in range(1, nd):
            arrived(rb_ref.at[i, k - 1], rb_recv.at[i, k - 1])
            total += rb_ref[i, k - 1].astype(f32)
        if i:
            s2_ref[i - 1] = total.astype(bf16)
            send(s2_ref.at[i - 1], ra_ref.at[i - 1], ra_send.at[i - 1], ra_recv.at[i - 1], d, ahead(i) * 2 + c)
        else:
            final = total
    for i in range(1, nz):
        arrived(ra_ref.at[i - 1], ra_recv.at[i - 1])
        final += ra_ref[i - 1].astype(f32)
    y_ref[...] = final.astype(bf16)
    for copy in sent + swaps:
        copy.wait_send()
    for put in puts:
        put.wait()


def body(tokens, route_weight, expert_ids, placement, pair_step, move_slot, expert_weights):
    nd = lax.axis_size("dp")
    nz = lax.axis_size("expert") // 2
    rows, width = tokens.shape
    slots, parts, _, hidden = expert_weights.shape
    bf16 = jnp.bfloat16
    vmem = pl.BlockSpec(memory_space=pltpu.VMEM)
    smem = pl.BlockSpec(memory_space=pltpu.SMEM)
    anywhere = pl.BlockSpec(memory_space=pl.ANY)
    dma = pltpu.SemaphoreType.DMA
    experts = placement.shape[0]
    full = width + 2 * (-(-experts // LANES) * LANES)
    blocks = nz * nd
    per = min(blocks, max(1, 256 // rows))
    return pl.pallas_call(
        functools.partial(layer_kernel, nd, nz),
        out_shape=(
            jax.ShapeDtypeStruct((rows, width), bf16),
            jax.ShapeDtypeStruct((1, parts, width, hidden), bf16),
        ),
        in_specs=[smem, smem, smem, vmem, vmem, vmem, anywhere],
        out_specs=(vmem, anywhere),
        scratch_shapes=[
            pltpu.VMEM((2, blocks, rows, full), bf16),
            pltpu.VMEM((per * rows, width), bf16),
            pltpu.VMEM((2, blocks * rows, slots * hidden), bf16),
            pltpu.VMEM((parts, width, hidden), bf16),
            pltpu.VMEM((parts, width, hidden), bf16),
            pltpu.VMEM((nz, nd, rows, width), bf16),
            pltpu.VMEM((nz, nd - 1, rows, width), bf16),
            pltpu.VMEM((nz - 1, rows, width), bf16),
            pltpu.VMEM((nz - 1, rows, width), bf16),
        ]
        + [pltpu.VMEM((slots, width, hidden), bf16)] * parts
        + [dma((slots, parts)), dma((parts,)), dma((parts,)), dma((parts,))]
        + [dma((nz - 1,))] * 2 + [dma((nz, nd - 1))] * 2 + [dma((nz,))] * 2
        + [dma((nz - 1,))] * 2 + [dma((nz, nd - 1))] * 2 + [dma((nz,))] * 2,
        compiler_params=pltpu.CompilerParams(
            collective_id=0, has_side_effects=True, vmem_limit_bytes=VMEM_LIMIT
        ),
        name="layer",
    )(placement, pair_step, move_slot, tokens, route_weight, expert_ids, expert_weights)


def solution(mesh):
    in_specs = (
        P(("dp", "expert"), None),
        P(("dp", "expert"), None),
        P(("dp", "expert"), None),
        P(),
        P(),
        P(),
        P("expert", None, None, "dp"),
    )
    out_specs = (P(("dp", "expert"), None), P("expert", None, None, "dp"))
    return jax.shard_map(body, mesh=mesh, in_specs=in_specs, out_specs=out_specs, check_vma=False)
```

time: 266 us -> 49.9 us (0.19)
  waiting for transfers between devices: 188 us -> 0 us
  Pallas kernels: 0 us -> 41.6 us
  between operations: 17.5 us -> 0.64 us
  local copies, waits for them, and re-layouts: 23.9 us -> 7.36 us
  matrix products: 13.8 us -> 0 us
  starting transfers between devices: 11.5 us -> 0 us
  other arithmetic: 10.9 us -> 0 us
    unnamed x3 -> x0, waiting for transfers between devices: 103 us -> none
    all_to_all x2 -> x0, waiting for transfers between devices: 44.2 us -> none  [the longest x1 26.6 us: body(): lax.all_to_all(summed, 'expert', split_axis=0, concat_axis=0, tiled=True)]
    pallas_call x0 -> x1, Pallas kernels: none -> 41.6 us  [body(): pl.pallas_call(functools.partial(layer_kernel, nd, nz), out_shape=(jax.Sh...]
    all_gather x1 -> x0, waiting for transfers between devices: 41.4 us -> none  [body(): lax.all_gather(arrived, 'dp', axis=0, tiled=True)]
    dot_general x3 -> x0, matrix products: 13.8 us -> none  [the longest x1 6.89 us: expert_partial(): jnp.einsum('ajcd,jkdh->ajckh', row_data, weights[:, :2], preferred_elemen...]
    all_to_all x2 -> x0, starting transfers between devices: 10.9 us -> none  [the longest x1 6.33 us: body(): lax.all_to_all(outgoing, 'expert', split_axis=0, concat_axis=0, tiled=True)]
    dynamic_update_slice x1 -> x0, other arithmetic: 9.08 us -> none  [body(): lax.dynamic_update_slice_in_dim(expert_weights, received, moving, 0)]
    dynamic_slice x3 -> x0, local copies, waits for them, and re-layouts: 7.07 us -> none  [the longest x1 5.9 us: body(): moving_block = lax.dynamic_slice_in_dim(expert_weights, moving, 1, 0)]
  transfers between devices with their start and end apart: 5 -> 0, of which waited for: 4 -> 0; matrix products, arithmetic and copies ran while one was open for 7% -> 0% of each run, Pallas kernels for 0% -> 0%
where the time goes in v4:
time: 49.9 us; the launch traced here: 49.7 us
  Pallas kernels  41.6 us (83%)
  local copies, waits for them, and re-layouts  7.36 us (15%)
  between operations  0.64 us (1%)
    pallas_call x1, Pallas kernels, body(): pl.pallas_call(functools.partial(layer_kernel, nd, nz), out_shape=(jax.Sh...  41.6 us
    unnamed x2, local copies, waits for them, and re-layouts  7.36 us

profile of v4, /device:TPU:0, one launch (start us, length us, event | category | flops | bytes accessed | tf_op | source)
XLA Modules:
  0.0 49.7 jit_solution(5514499113072284908)
XLA Ops:
  0.6 41.6 %layer.1 = (bf16[8,4096]{1,0:T(8,128)(2,1)}, bf16[1,3,4096,256]{3,2,1,0:T(8,128)(2,1)}) custom-call(s32[16]{0:T(128)} %place_ref.1, s32[8]{0:T(128)} %step_ref.1, s32[8]{0:T(128)} %mv_ref.1, bf16[8,4096]{1,0:T(8,128)(2,1)} %x_ref.1, f32[8,8]{1,0:T(8,128)} %rw_ref.1, s32[8,8]{1,0:T(8,128)} %id_ref.1, bf16[2,3,4096,256]{3,2,1,0:T(8,128)(2,1)} %w_hbm.1), custom_call_target="tpu_custom_call" | custom-call | tf_op jit(solution)/shard_map/layer/pallas_call | solution.py:263
  42.3 1.5 %copy.11 = bf16[8,4096]{1,0:T(8,128)(2,1)} copy(bf16[8,4096]{1,0:T(8,128)(2,1)} %get-tuple-element.4) | data formatting | bytes 131072
  43.8 5.9 %copy.12 = bf16[1,3,4096,256]{3,2,1,0:T(8,128)(2,1)} copy(bf16[1,3,4096,256]{3,2,1,0:T(8,128)(2,1)} %get-tuple-element.5) | data formatting | bytes 12582912

commit v5 on v4

--- a/solution.py
+++ b/solution.py
@@ -9,7 +9,7 @@
 
 MESH = pl.DeviceIdType.MESH
 LANES = 128
-VMEM_LIMIT = 56 * 1024 * 1024
+VMEM_LIMIT = 52 * 1024 * 1024
 
 
 def place(nd, nz):
@@ -40,7 +40,7 @@
 
 
 def layer_kernel(
-    nd, nz, place_ref, step_ref, mv_ref, x_ref, rw_ref, id_ref, w_hbm, y_ref, moved_hbm,
+    nd, nz, place_ref, step_ref, mv_ref, x_ref, rw_ref, id_ref, w_hbm, y_ref, moved_ref,
     g_ref, t_ref, h_ref, out_ref, got_ref, rc_ref, rb_ref, s2_ref, ra_ref, *rest,
 ):
     d, zz, c, e = place(nd, nz)
@@ -48,7 +48,7 @@
     f32, bf16 = jnp.float32, jnp.bfloat16
     slots, parts, width, hidden = w_hbm.shape
     w_refs = rest[:parts]
-    (w_sem, o_sem, s_send, s_recv, a_send, a_recv, b_send, b_recv, c_send, c_recv,
+    (w_sem, s_send, s_recv, a_send, a_recv, b_send, b_recv, c_send, c_recv,
      ra_send, ra_recv, rb_send, rb_recv, rc_send, rc_recv) = rest[parts:]
     tokens, lanes = x_ref.shape[0], (g_ref.shape[3] - width) // 2
     loads = [
@@ -214,17 +214,13 @@
                 send(rc_ref.at[i, pd], rb_ref.at[i, k - 1], rb_send.at[i, k - 1], rb_recv.at[i, k - 1], pd, e)
     first = e // 2 * 2
     swapping = step_ref[first] + step_ref[first + 1] > 0
-    puts = []
     for m in range(parts):
         swaps[m].wait_recv()
 
         def one(at):
-            got_ref[m, at, :] = lax.select(swapping, got_ref[m, at, :], out_ref[m, at, :])
+            moved_ref[0, m, at, :] = lax.select(swapping, got_ref[m, at, :], out_ref[m, at, :])
 
         rows_loop(one)
-        put = pltpu.make_async_copy(got_ref.at[m], moved_hbm.at[0, m], o_sem.at[m])
-        put.start()
-        puts.append(put)
     final = None
     for i in order:
         total = rc_ref[i, d].astype(f32)
@@ -242,8 +238,6 @@
     y_ref[...] = final.astype(bf16)
     for copy in sent + swaps:
         copy.wait_send()
-    for put in puts:
-        put.wait()
 
 
 def body(tokens, route_weight, expert_ids, placement, pair_step, move_slot, expert_weights):
@@ -264,10 +258,10 @@
         functools.partial(layer_kernel, nd, nz),
         out_shape=(
             jax.ShapeDtypeStruct((rows, width), bf16),
-            jax.ShapeDtypeStruct((1, parts, width, hidden), bf16),
+            pltpu.VMEM((1, parts, width, hidden), bf16),
         ),
         in_specs=[smem, smem, smem, vmem, vmem, vmem, anywhere],
-        out_specs=(vmem, anywhere),
+        out_specs=(vmem, vmem),
         scratch_shapes=[
             pltpu.VMEM((2, blocks, rows, full), bf16),
             pltpu.VMEM((per * rows, width), bf16),
@@ -280,7 +274,7 @@
             pltpu.VMEM((nz - 1, rows, width), bf16),
         ]
         + [pltpu.VMEM((slots, width, hidden), bf16)] * parts
-        + [dma((slots, parts)), dma((parts,)), dma((parts,)), dma((parts,))]
+        + [dma((slots, parts)), dma((parts,)), dma((parts,))]
         + [dma((nz - 1,))] * 2 + [dma((nz, nd - 1))] * 2 + [dma((nz,))] * 2
         + [dma((nz - 1,))] * 2 + [dma((nz, nd - 1))] * 2 + [dma((nz,))] * 2,
         compiler_params=pltpu.CompilerParams(

time: 49.9 us -> 45.8 us (0.918)
  local copies, waits for them, and re-layouts: 7.36 us -> 3.34 us
    unnamed x2 -> x4, local copies, waits for them, and re-layouts: 7.36 us -> 3.34 us
where the time goes in v5:
time: 45.8 us; the launch traced here: 45.6 us
  Pallas kernels  41.6 us (91%)
  local copies, waits for them, and re-layouts  3.34 us (7%)
  between operations  0.65 us (1%)
    pallas_call x1, Pallas kernels, body(): pl.pallas_call(functools.partial(layer_kernel, nd, nz), out_shape=(jax.Sh...  41.6 us
    unnamed x4, local copies, waits for them, and re-layouts  3.34 us

profile of v5, /device:TPU:0, one launch (start us, length us, event | category | flops | bytes accessed | tf_op | source)
XLA Modules:
  0.0 45.6 jit_solution(11064006117290326718)
XLA Ops:
  0.6 41.6 %layer.1 = (bf16[8,4096]{1,0:T(8,128)(2,1)}, bf16[1,3,4096,256]{3,2,1,0:T(8,128)(2,1)S(1)}) custom-call(s32[16]{0:T(128)} %place_ref.1, s32[8]{0:T(128)} %step_ref.1, s32[8]{0:T(128)} %mv_ref.1, bf16[8,4096]{1,0:T(8,128)(2,1)} %x_ref.1, f32[8,8]{1,0:T(8,128)} %rw_ref.1, s32[8,8]{1,0:T(8,128)} %id_ref.1, bf16[2,3,4096,256]{3,2,1,0:T(8,128)(2,1)} %w_hbm.1), custom_call_target="tpu_custom_call" | custom-call | tf_op jit(solution)/shard_map/layer/pallas_call | solution.py:257
  42.3 0.0 copy-start
  42.3 2.7 %copy.11 = bf16[1,3,4096,256]{3,2,1,0:T(8,128)(2,1)} copy(bf16[1,3,4096,256]{3,2,1,0:T(8,128)(2,1)S(1)} %get-tuple-element.3) | data formatting | bytes 12582912
  45.0 0.0 copy-done
  45.0 0.6 %copy.12 = bf16[8,4096]{1,0:T(8,128)(2,1)} copy(bf16[8,4096]{1,0:T(8,128)(2,1)S(1)} %copy-done) | data formatting | bytes 131072
Async XLA Ops:
  42.3 2.7 %copy-start = (bf16[8,4096]{1,0:T(8,128)(2,1)S(1)}, bf16[8,4096]{1,0:T(8,128)(2,1)}, u32[]{:S(2)}) copy-start(bf16[8,4096]{1,0:T(8,128)(2,1)} %get-tuple-element.6) | copy-start | bytes 196612
